TPU v7x, 32 devices: a whole 2x2x4 slice. The times are simulated.
32 devices in a mesh: scene: 4 (over x, core), seq: 8 (over z, y).
Axes of the slice: x: 2, y: 2, z: 4, core: 2. Of those that a mesh axis runs over, the one named last changes fastest.
Arguments:
- tokens: bfloat16 [10240, 768], P(('scene', 'seq')), may hold values from -6 to 6
- scene_tokens: int32 [4], P('scene'), may hold values from 128 to 320, as said below
- cotangent: bfloat16 [10240, 768], P(('scene', 'seq')), may hold values from -6 to 6
- qkv_master: float32 [768, 2304], P(('scene', 'seq')), may hold values from -0.21875 to 0.21875
- out_master: float32 [768, 768], P(('scene', 'seq')), may hold values from -6 to 6
- up_master: float32 [768, 3072], P(('scene', 'seq')), may hold values from -0.21875 to 0.21875
- down_master: float32 [3072, 768], P(('scene', 'seq')), may hold values from -0.109375 to 0.109375
- gain_one: float32 [768], replicated, may hold values from 0.5 to 1.5
- gain_two: float32 [768], replicated, may hold values from 0.5 to 1.5
Outputs:
- mixed: bfloat16 [10240, 768], P(('scene', 'seq'))
- input_grad: float32 [10240, 768], P(('scene', 'seq'))
- qkv_grad: float32 [768, 2304], P(('scene', 'seq'))
- out_grad: float32 [768, 768], P(('scene', 'seq'))
- up_grad: float32 [768, 3072], P(('scene', 'seq'))
- down_grad: float32 [3072, 768], P(('scene', 'seq'))
- gain_one_grad: float32 [768], P(('scene', 'seq'))
- gain_two_grad: float32 [768], P(('scene', 'seq'))
Inputs may be any that keep to these rules, and one draw needn't show every extreme that they name: Slots 0 to scene_tokens[s] - 1 of every device of scene s's group hold that scene's tokens, the others are padding; one scene, drawn from the seed, has all 320 slots of every device live.
All inputs are finite; a program needn't handle non-finite values.
Results may differ from a plain program's by a relative error of at most 0.02.
Values may be sent and summed in bfloat16 or wider, within the bound.
No kernel may reach another device: no remote copies, remote signals or barrier semaphores. Data moves between devices by JAX's collectives and lax.ppermute only.
A program may use at most 512 MiB of HBM per device.

v0:
```python
import jax
import jax.numpy as jnp
from jax import lax
from jax.sharding import PartitionSpec as P

HEADS = 12
HEAD = 64
NEG_BIG = -1e30


def norm_rows(values, gain_vector):
    mean_value = jnp.mean(values, axis=-1, keepdims=True)
    centered = values - mean_value
    variance = jnp.mean(centered * centered, axis=-1, keepdims=True)
    inverse = lax.rsqrt(variance + 1e-05)
    scaled = centered * inverse
    return (scaled * gain_vector, scaled, inverse)


def norm_back(grad_result, scaled, inverse, gain_vector):
    grad_scaled = grad_result * gain_vector
    first_mean = jnp.mean(grad_scaled, axis=-1, keepdims=True)
    second_mean = jnp.mean(grad_scaled * scaled, axis=-1, keepdims=True)
    grad_input = inverse * (grad_scaled - first_mean - scaled * second_mean)
    return (grad_input, jnp.sum(grad_result * scaled, axis=0))


def split_heads(values):
    return values.reshape(values.shape[0], HEADS, HEAD)


def score_grads(query_part, grad_part, key_part, value_part, lse_part, delta_part, live_keys):
    scores = (
        jnp.einsum("qhd,khd->hqk", query_part, key_part, preferred_element_type=jnp.float32) * 0.125
    )
    weights_now = jnp.where(live_keys[None, None, :], jnp.exp(scores - lse_part[:, :, None]), 0.0)
    grad_weights = jnp.einsum(
        "qhd,khd->hqk", grad_part, value_part, preferred_element_type=jnp.float32
    )
    dscore = (weights_now * (grad_weights - delta_part[:, :, None])).astype(jnp.bfloat16)
    return (weights_now.astype(jnp.bfloat16), dscore)


def on_device(
    tokens,
    scene_tokens,
    cotangent,
    qkv_master,
    out_master,
    up_master,
    down_master,
    gain_one,
    gain_two,
):
    local_rows = tokens.shape[0]
    model_width = tokens.shape[1]
    live_count = scene_tokens[0]
    local_live = jnp.arange(local_rows, dtype=jnp.int32) < live_count
    qkv_part = qkv_master.astype(jnp.bfloat16)
    out_part = out_master.astype(jnp.bfloat16)
    up_part = up_master.astype(jnp.bfloat16)
    down_part = down_master.astype(jnp.bfloat16)
    qkv_weight, out_weight, up_weight, down_weight = (
        lax.all_gather(qkv_part, ("scene", "seq"), axis=0, tiled=True),
        lax.all_gather(out_part, ("scene", "seq"), axis=0, tiled=True),
        lax.all_gather(up_part, ("scene", "seq"), axis=0, tiled=True),
        lax.all_gather(down_part, ("scene", "seq"), axis=0, tiled=True),
    )
    inputs = tokens.astype(jnp.float32)
    normed_one, scaled_one, inverse_one = norm_rows(inputs, gain_one)
    normed_low = normed_one.astype(jnp.bfloat16)
    qkv_rows = jnp.dot(normed_low, qkv_weight, preferred_element_type=jnp.float32).astype(
        jnp.bfloat16
    )
    queries = qkv_rows[:, :model_width]
    key_rows = qkv_rows[:, model_width : 2 * model_width]
    value_rows = qkv_rows[:, 2 * model_width :]
    query_heads = split_heads(queries)

    def piece_live(piece_rows):
        places = jnp.arange(piece_rows, dtype=jnp.int32)
        return places % local_rows < live_count

    row_max = jnp.full((HEADS, local_rows), NEG_BIG, jnp.float32)
    key_piece = lax.all_gather(key_rows, "seq", axis=0, tiled=True)
    value_piece = lax.all_gather(value_rows, "seq", axis=0, tiled=True)
    piece_rows = key_piece.shape[0]
    scores = (
        jnp.einsum(
            "qhd,khd->hqk", query_heads, split_heads(key_piece), preferred_element_type=jnp.float32
        )
        * 0.125
    )
    scores = jnp.where(piece_live(piece_rows)[None, None, :], scores, NEG_BIG)
    new_max = jnp.maximum(row_max, jnp.max(scores, axis=-1))
    exponent = jnp.exp(scores - new_max[:, :, None])
    new_sum = jnp.sum(exponent, axis=-1)
    update = jnp.einsum(
        "hqk,khd->hqd",
        exponent.astype(jnp.bfloat16),
        split_heads(value_piece),
        preferred_element_type=jnp.float32,
    )
    row_lse = new_max + jnp.log(new_sum)
    attended = (
        (update / new_sum[:, :, None])
        .transpose(1, 0, 2)
        .reshape(local_rows, model_width)
        .astype(jnp.bfloat16)
    )
    resid = inputs + jnp.dot(attended, out_weight, preferred_element_type=jnp.float32)
    normed_two, scaled_two, inverse_two = norm_rows(resid, gain_two)
    normed_two_low = normed_two.astype(jnp.bfloat16)
    upper = jnp.dot(normed_two_low, up_weight, preferred_element_type=jnp.float32)
    activated, gelu_back = jax.vjp(jax.nn.gelu, upper)
    activated_low = activated.astype(jnp.bfloat16)
    mixed = (
        resid + jnp.dot(activated_low, down_weight, preferred_element_type=jnp.float32)
    ).astype(jnp.bfloat16)
    grad_result = cotangent.astype(jnp.float32) * local_live[:, None].astype(jnp.float32)
    grad_low = grad_result.astype(jnp.bfloat16)
    down_grad = jnp.einsum("tf,td->fd", activated_low, grad_low, preferred_element_type=jnp.float32)
    grad_active = jnp.einsum("td,fd->tf", grad_low, down_weight, preferred_element_type=jnp.float32)
    grad_upper = gelu_back(grad_active)[0].astype(jnp.bfloat16)
    up_grad = jnp.einsum(
        "td,tf->df", normed_two_low, grad_upper, preferred_element_type=jnp.float32
    )
    grad_normed_two = jnp.einsum(
        "tf,df->td", grad_upper, up_weight, preferred_element_type=jnp.float32
    )
    grad_norm_second, gain_two_grad = norm_back(grad_normed_two, scaled_two, inverse_two, gain_two)
    grad_resid = grad_result + grad_norm_second
    grad_branch = grad_resid.astype(jnp.bfloat16)
    out_grad = jnp.einsum("te,td->ed", attended, grad_branch, preferred_element_type=jnp.float32)
    grad_attended = jnp.einsum(
        "td,ed->te", grad_branch, out_weight, preferred_element_type=jnp.float32
    ).astype(jnp.bfloat16)
    grad_heads = split_heads(grad_attended)
    delta = jnp.sum(
        grad_heads.astype(jnp.float32) * split_heads(attended).astype(jnp.float32), axis=-1
    ).T
    total_rows = local_rows * lax.axis_size("seq")
    key_piece = lax.all_gather(key_rows, "seq", axis=0, tiled=True)
    value_piece = lax.all_gather(value_rows, "seq", axis=0, tiled=True)
    piece_rows = key_piece.shape[0]
    key_heads = split_heads(key_piece)
    weights_low, dscore = score_grads(
        query_heads,
        grad_heads,
        key_heads,
        split_heads(value_piece),
        row_lse,
        delta,
        piece_live(piece_rows),
    )
    grad_query = (
        jnp.einsum("hqk,khd->qhd", dscore, key_heads, preferred_element_type=jnp.float32) * 0.125
    )
    key_terms = (
        jnp.einsum("hqk,qhd->khd", dscore, query_heads, preferred_element_type=jnp.float32) * 0.125
    )
    value_terms = jnp.einsum(
        "hqk,qhd->khd", weights_low, grad_heads, preferred_element_type=jnp.float32
    )
    key_buffer = key_terms
    value_buffer = value_terms
    grad_query, key_buffer, value_buffer = (grad_query, key_buffer, value_buffer)
    grad_keys, grad_values = (
        lax.psum_scatter(
            key_buffer.reshape(total_rows, model_width).astype(jnp.bfloat16),
            "seq",
            scatter_dimension=0,
            tiled=True,
        ).astype(jnp.float32),
        lax.psum_scatter(
            value_buffer.reshape(total_rows, model_width).astype(jnp.bfloat16),
            "seq",
            scatter_dimension=0,
            tiled=True,
        ).astype(jnp.float32),
    )
    grad_qkv = jnp.concatenate(
        [grad_query.reshape(local_rows, model_width), grad_keys, grad_values], axis=1
    ).astype(jnp.bfloat16)
    qkv_grad = jnp.einsum("td,te->de", normed_low, grad_qkv, preferred_element_type=jnp.float32)
    grad_normed_one = jnp.einsum(
        "te,de->td", grad_qkv, qkv_weight, preferred_element_type=jnp.float32
    )
    grad_norm_first, gain_one_grad = norm_back(grad_normed_one, scaled_one, inverse_one, gain_one)
    input_grad = grad_resid + grad_norm_first
    qkv_share, out_share, up_share, down_share, first_share, second_share = (
        lax.psum_scatter(qkv_grad, ("scene", "seq"), scatter_dimension=0, tiled=True),
        lax.psum_scatter(out_grad, ("scene", "seq"), scatter_dimension=0, tiled=True),
        lax.psum_scatter(up_grad, ("scene", "seq"), scatter_dimension=0, tiled=True),
        lax.psum_scatter(down_grad, ("scene", "seq"), scatter_dimension=0, tiled=True),
        lax.psum_scatter(gain_one_grad, ("scene", "seq"), scatter_dimension=0, tiled=True),
        lax.psum_scatter(gain_two_grad, ("scene", "seq"), scatter_dimension=0, tiled=True),
    )
    return (
        mixed,
        input_grad,
        qkv_share,
        out_share,
        up_share,
        down_share,
        first_share,
        second_share,
    )


def solution(mesh):
    in_specs = (
        P(("scene", "seq"), None),
        P("scene"),
        P(("scene", "seq"), None),
        P(("scene", "seq"), None),
        P(("scene", "seq"), None),
        P(("scene", "seq"), None),
        P(("scene", "seq"), None),
        P(),
        P(),
    )
    out_specs = (
        P(("scene", "seq"), None),
        P(("scene", "seq"), None),
        P(("scene", "seq"), None),
        P(("scene", "seq"), None),
        P(("scene", "seq"), None),
        P(("scene", "seq"), None),
        P(("scene", "seq")),
        P(("scene", "seq")),
    )
    return jax.shard_map(
        on_device, mesh=mesh, in_specs=in_specs, out_specs=out_specs, check_vma=False
    )
```

profile of v0, /device:TPU:0, one launch (start us, length us, event | category | flops | bytes accessed | tf_op | source)
XLA Modules:
  0.0 1135.8 jit_solution(7848209360860348284)
XLA Ops:
  11.4 63.0 %all-gather.7.cloned.1.call-done = bf16[768,2304]{1,0:T(8,128)(2,1)} async-done(((bf16[24,2304]{1,0:T(8,128)(2,1)}), bf16[768,2304]{1,0:T(8,128)(2,1)}) %all-gather.7.cloned.1.call-update) | async-done | bytes 3538960 | tf_op jit(solution)/shard_map/all_gather | solution.py:64
  74.4 3.6 convolution_convert_fusion
  83.1 65.0 %all-gather.9.cloned.1.call-done = bf16[2560,768]{1,0:T(8,128)(2,1)} async-done(((bf16[320,768]{1,0:T(8,128)(2,1)}), bf16[2560,768]{1,0:T(8,128)(2,1)}) %all-gather.9.cloned.1.call-update) | async-done | bytes 3932176 | tf_op jit(solution)/shard_map/all_gather | solution.py:85
  148.1 6.3 copy.29
  154.4 17.1 %select_reduce_fusion = (f32[12,320]{1,0:T(8,128)S(1)}, f32[12,320,2560]{2,1,0:T(8,128)}) fusion(pred[2560]{0:T(1024)(128)(4,1)S(1)} %fusion.51, bf16[320,12,64]{0,2,1:T(8,128)(2,1)S(1)} %bitcast.50, bf16[2560,12,64]{0,2,1:T(8,128)(2,1)} %bitcast.47), kind=kOutput, calls=%fused_computation.3 | convolution fusion | flops 1287778560 | bytes 43763200 | tf_op jit(solution)/shard_map/qhd,khd->hqk/dot_general | solution.py:89
  171.5 47.9 %all-gather.11.cloned.1.call-done = bf16[2560,768]{1,0:T(8,128)(2,1)} async-done(((bf16[320,768]{1,0:T(8,128)(2,1)}), bf16[2560,768]{1,0:T(8,128)(2,1)}) %all-gather.11.cloned.1.call-update) | async-done | bytes 3932176 | tf_op jit(solution)/shard_map/all_gather | solution.py:86
  219.4 6.2 copy.30
  225.6 18.1 %fusion = f32[12,320]{1,0:T(8,128)S(1)} fusion(f32[12,320,2560]{2,1,0:T(8,128)} %get-tuple-element.20, f32[12,320]{1,0:T(8,128)S(1)} %broadcast_maximum_fusion, pred[2560]{0:T(1024)(128)(4,1)S(1)} %fusion.51), kind=kLoop, calls=%fused_computation.4 | loop fusion | flops 39317760 | bytes 39354880 | tf_op jit(solution)/shard_map/reduce_sum | solution.py:97
  243.8 15.2 %divide_convert_fusion = bf16[320,12,64]{0,2,1:T(8,128)(2,1)S(1)} fusion(bf16[2560,12,64]{0,2,1:T(8,128)(2,1)S(1)} %bitcast.55, f32[12,320,2560]{2,1,0:T(8,128)} %get-tuple-element.20, f32[12,320]{1,0:T(8,128)S(1)} %broadcast_maximum_fusion, pred[2560]{0:T(1024)(128)(4,1)S(1)} %fusion.51, f32[320,12]{0,1:T(8,128)S(1)} %bitcast.62), kind=kOutput, calls=%fused_computation.35 | convolution fusion | flops 1298104320 | bytes 43778560 | tf_op jit(solution)/shard_map/hqk,khd->hqd/dot_general | solution.py:98
  259.0 16.4 %all-gather.13.cloned.1.call-done = bf16[768,768]{1,0:T(8,128)(2,1)} async-done(((bf16[24,768]{1,0:T(8,128)(2,1)}), bf16[768,768]{1,0:T(8,128)(2,1)}) %all-gather.13.cloned.1.call-update) | async-done | bytes 1179664 | tf_op jit(solution)/shard_map/all_gather | solution.py:65
  278.2 63.0 %all-gather.15.cloned.1.call-done = bf16[768,3072]{1,0:T(8,128)(2,1)} async-done(((bf16[24,3072]{1,0:T(8,128)(2,1)}), bf16[768,3072]{1,0:T(8,128)(2,1)}) %all-gather.15.cloned.1.call-update) | async-done | bytes 4718608 | tf_op jit(solution)/shard_map/all_gather | solution.py:66
  341.3 6.0 fusion.65
  347.3 59.8 %all-gather.17.cloned.1.call-done = bf16[3072,768]{1,0:T(8,128)(2,1)} async-done(((bf16[96,768]{1,0:T(8,128)(2,1)}), bf16[3072,768]{1,0:T(8,128)(2,1)}) %all-gather.17.cloned.1.call-update) | async-done | bytes 4718608 | tf_op jit(solution)/shard_map/all_gather | solution.py:67
  407.1 7.8 fusion.18
  415.0 2.5 multiply_reduce_fusion.1
  419.5 18.2 %fusion.9 = bf16[12,64,2560]{2,1,0:T(8,128)(2,1)} fusion(bf16[320,12,64]{0,2,1:T(8,128)(2,1)} %bitcast.59, f32[12,320,2560]{2,1,0:T(8,128)} %get-tuple-element.20, f32[12,320]{1,0:T(8,128)} %log_add_fusion, pred[2560]{0:T(1024)(128)(4,1)S(1)} %fusion.51), kind=kOutput, calls=%fused_computation.14 | convolution fusion | flops 1299578880 | bytes 43763200 | tf_op jit(solution)/shard_map/hqk,qhd->khd/dot_general | solution.py:162
  437.7 6.3 copy.34
  445.6 26.5 %multiply_convert_fusion = bf16[12,320,2560]{2,1,0:T(8,128)(2,1)} fusion(f32[12,320,2560]{2,1,0:T(8,128)} %get-tuple-element.20, bf16[320,12,64]{0,2,1:T(8,128)(2,1)} %bitcast.61, bf16[2560,12,64]{0,2,1:T(8,128)(2,1)} %bitcast.54, f32[12,320]{1,0:T(8,128)S(1)} %bitcast.63, f32[12,320]{1,0:T(8,128)S(1)} %copy-done.19, pred[2560]{0:T(1024)(128)(4,1)S(1)} %fusion.51), kind=kOutput, calls=%fused_computation | convolution fusion | flops 1317273600 | bytes 63439360 | tf_op jit(solution)/shard_map/qhd,khd->hqk/dot_general | solution.py:37
  472.1 12.6 %multiply_convert_fusion.1 = bf16[12,64,2560]{2,1,0:T(8,128)(2,1)} fusion(bf16[320,12,64]{0,2,1:T(8,128)(2,1)S(1)} %bitcast.51, bf16[12,320,2560]{2,1,0:T(8,128)(2,1)} %multiply_convert_fusion), kind=kOutput, calls=%fused_computation.11 | convolution fusion | flops 1262223360 | bytes 24084480 | tf_op jit(solution)/shard_map/hqk,qhd->khd/dot_general | solution.py:160
  484.7 6.3 copy.32
  494.3 6.8 fusion.64
  502.2 8.7 fusion.45
  511.0 10.9 fusion.23
  522.0 5.4 reduce-scatter.21.cloned.1.call-done
  529.5 86.1 %reduce-scatter.19.cloned.1.call-done = bf16[320,768]{1,0:T(8,128)(2,1)} async-done(((bf16[2560,768]{1,0:T(8,128)(2,1)}), bf16[320,768]{1,0:T(8,128)(2,1)}) %reduce-scatter.19.cloned.1.call-update) | async-done | bytes 491536
  617.7 6.4 fusion.38
  624.1 6.9 fusion.22
  632.9 40.4 %all-reduce.2 = (f32[768]{0:T(1024)S(1)}, f32[768]{0:T(1024)S(1)}) all-reduce(f32[768]{0:T(1024)S(1)} %get-tuple-element.10, f32[768]{0:T(1024)S(1)} %copy-done.23), channel_id=8, replica_groups=mesh['scene'=4,'seq'=8] {'scene','seq'}, use_global_device_ids=true, to_apply=%region_18.19.clone | all-reduce | flops 1536 | bytes 12288
  675.8 44.5 %reduce-scatter.13.cloned.1.call-done = f32[24,768]{1,0:T(8,128)} async-done(((f32[768,768]{1,0:T(8,128)}), f32[24,768]{1,0:T(8,128)}) %reduce-scatter.13.cloned.1.call-update) | async-done | bytes 73744 | tf_op jit(solution)/shard_map/reduce_scatter | solution.py:193
  720.3 142.0 %reduce-scatter.15.cloned.1.call-done = f32[24,3072]{1,0:T(8,128)} async-done(((f32[768,3072]{1,0:T(8,128)}), f32[24,3072]{1,0:T(8,128)}) %reduce-scatter.15.cloned.1.call-update) | async-done | bytes 294928 | tf_op jit(solution)/shard_map/reduce_scatter | solution.py:194
  862.3 141.0 %reduce-scatter.17.cloned.1.call-done = f32[96,768]{1,0:T(8,128)} async-done(((f32[3072,768]{1,0:T(8,128)}), f32[96,768]{1,0:T(8,128)}) %reduce-scatter.17.cloned.1.call-update) | async-done | bytes 294928 | tf_op jit(solution)/shard_map/reduce_scatter | solution.py:195
  1003.3 125.4 %reduce-scatter.11.cloned.1.call-done = f32[24,2304]{1,0:T(8,128)} async-done(((f32[768,2304]{1,0:T(8,128)}), f32[24,2304]{1,0:T(8,128)}) %reduce-scatter.11.cloned.1.call-update) | async-done | bytes 221200 | tf_op jit(solution)/shard_map/reduce_scatter | solution.py:192
  (108 shorter events, 27.9 us)
Async XLA Ops:
  7.2 67.2 %all-gather.7.cloned.1.call-start = ((), (), s32[]{:S(2)}) async-start(), calls=%async_computation.6 | async-start | bytes 3649536 | tf_op jit(solution)/shard_map/all_gather | solution.py:64
  8.8 139.3 %all-gather.9.cloned.1.call-start = ((), (), s32[]{:S(2)}) async-start(), calls=%async_computation.7 | async-start | bytes 4423680 | tf_op jit(solution)/shard_map/all_gather | solution.py:85
  10.1 64.3 %copy-start.15 = (f32[320]{0:T(512)}, f32[320]{0:T(512)S(1)}, u32[]{:S(2)}) copy-start(f32[320]{0:T(512)S(1)} %broadcast_multiply_fusion.5) | copy-start | bytes 3844
  11.4 63.0 %copy-start.17 = (f32[320]{0:T(512)}, f32[320]{0:T(512)S(1)}, u32[]{:S(2)}) copy-start(f32[320]{0:T(512)S(1)} %add_rsqrt_fusion.1) | copy-start | bytes 3844
  78.0 2.6 copy-start.10
  78.0 3.3 copy-start.11
  79.1 140.3 %all-gather.11.cloned.1.call-start = ((), (), s32[]{:S(2)}) async-start(), calls=%async_computation.8 | async-start | bytes 4423680 | tf_op jit(solution)/shard_map/all_gather | solution.py:86
  79.8 195.6 %all-gather.13.cloned.1.call-start = ((), (), s32[]{:S(2)}) async-start(), calls=%async_computation.9 | async-start | bytes 1216512 | tf_op jit(solution)/shard_map/all_gather | solution.py:65
  80.5 260.8 %all-gather.15.cloned.1.call-start = ((), (), s32[]{:S(2)}) async-start(), calls=%async_computation.10 | async-start | bytes 4866048 | tf_op jit(solution)/shard_map/all_gather | solution.py:66
  81.3 325.8 %all-gather.17.cloned.1.call-start = ((), (), s32[]{:S(2)}) async-start(), calls=%async_computation.11 | async-start | bytes 4866048 | tf_op jit(solution)/shard_map/all_gather | solution.py:67
  82.0 445.4 %reduce-scatter.21.cloned.1.call-start = ((), (), s32[]{:S(2)}) async-start(), calls=%async_computation.17 | async-start | bytes 4423680
  82.8 324.4 %copy-start.20 = (f32[320]{0:T(512)}, f32[320]{0:T(512)S(1)}, u32[]{:S(2)}) copy-start(f32[320]{0:T(512)S(1)} %fusion.55) | copy-start | bytes 3844
  225.6 18.1 %copy-start.4 = (bf16[2560,768]{0,1:T(8,128)(2,1)S(1)}, bf16[2560,768]{0,1:T(8,128)(2,1)}, u32[]{:S(2)}) copy-start(bf16[2560,768]{0,1:T(8,128)(2,1)} %copy.30) | copy-start | bytes 11796484
  243.7 31.6 %copy-start = (bf16[320,768]{1,0:T(8,128)(2,1)S(1)}, bf16[320,768]{1,0:T(8,128)(2,1)}, u32[]{:S(2)}) copy-start(bf16[320,768]{1,0:T(8,128)(2,1)} %param.9) | copy-start | bytes 1474564
  259.0 88.3 %copy-start.1 = (bf16[320,12,64]{0,2,1:T(8,128)(2,1)}, bf16[320,12,64]{0,2,1:T(8,128)(2,1)S(1)}, u32[]{:S(2)}) copy-start(bf16[320,12,64]{0,2,1:T(8,128)(2,1)S(1)} %divide_convert_fusion) | copy-start | bytes 1474564
  259.0 82.3 %copy-start.12 = (f32[768]{0:T(1024)S(1)}, f32[768]{0:T(1024)}, u32[]{:S(2)}) copy-start(f32[768]{0:T(1024)} %param.17) | copy-start | bytes 9220
  278.2 128.9 %copy-start.8 = (bf16[320,768]{1,0:T(8,128)(2,1)S(1)}, bf16[320,768]{1,0:T(8,128)(2,1)}, u32[]{:S(2)}) copy-start(bf16[320,768]{1,0:T(8,128)(2,1)} %param.11) | copy-start | bytes 1474564
  407.1 7.8 copy-start.24
  415.0 2.5 copy-start.7
  415.0 2.5 copy-start.21
  415.0 2.9 copy-start.3
  444.1 171.5 %reduce-scatter.19.cloned.1.call-start = ((), (), s32[]{:S(2)}) async-start(), calls=%async_computation.16 | async-start | bytes 4423680
  491.0 229.3 %reduce-scatter.13.cloned.1.call-start = ((), (), s32[]{:S(2)}) async-start(), calls=%async_computation.13 | async-start | bytes 2433024 | tf_op jit(solution)/shard_map/reduce_scatter | solution.py:193
  494.3 368.1 %reduce-scatter.15.cloned.1.call-start = ((), (), s32[]{:S(2)}) async-start(), calls=%async_computation.14 | async-start | bytes 9732096 | tf_op jit(solution)/shard_map/reduce_scatter | solution.py:194
  501.2 502.1 %reduce-scatter.17.cloned.1.call-start = ((), (), s32[]{:S(2)}) async-start(), calls=%async_computation.15 | async-start | bytes 9732096 | tf_op jit(solution)/shard_map/reduce_scatter | solution.py:195
  511.0 106.7 %copy-start.13 = (f32[768]{0:T(1024)S(1)}, f32[768]{0:T(1024)}, u32[]{:S(2)}) copy-start(f32[768]{0:T(1024)} %param.16) | copy-start | bytes 9220
  511.0 106.7 %copy-start.16 = (f32[320]{0:T(512)S(1)}, f32[320]{0:T(512)}, u32[]{:S(2)}) copy-start(f32[320]{0:T(512)} %copy-done.15) | copy-start | bytes 3844
  511.0 106.7 %copy-start.18 = (f32[320]{0:T(512)S(1)}, f32[320]{0:T(512)}, u32[]{:S(2)}) copy-start(f32[320]{0:T(512)} %copy-done.17) | copy-start | bytes 3844
  511.0 617.7 %reduce-scatter.11.cloned.1.call-start = ((), (), s32[]{:S(2)}) async-start(), calls=%async_computation.12 | async-start | bytes 7299072 | tf_op jit(solution)/shard_map/reduce_scatter | solution.py:192
  624.1 6.9 copy-start.5
  624.1 6.9 copy-start.6
  624.1 6.9 copy-start.25
  (6 other events, 8.5 us)
Sparse Core Ops, SparseCore 0:
  11.5 62.8 all-gather.6
  79.2 68.8 all-gather.8
  150.9 68.4 all-gather.10
  222.7 52.6 all-gather.12
  278.7 62.5 all-gather.14
  344.6 62.4 all-gather.16
  444.2 83.1 reduce-scatter.20
  531.5 83.9 reduce-scatter.18
  621.4 98.8 reduce-scatter.12
  727.6 134.6 reduce-scatter.14
  868.8 134.4 reduce-scatter.16
  1010.4 118.2 reduce-scatter.10
where the time goes:
time: 1150 us; the launch traced here: 1140 us
  waiting for transfers between devices  860 us (75%)
  matrix products  156 us (14%)
  blocking collectives  40.4 us (4%)
  local copies, waits for them, and re-layouts  35 us (3%)
  other arithmetic  28.3 us (2%)
  between operations  15.4 us (1%)
    reduce_scatter x1, waiting for transfers between devices, on_device(): lax.psum_scatter(up_grad, ('scene', 'seq'), scatter_dimension=0, tiled=True)  142 us
    reduce_scatter x1, waiting for transfers between devices, on_device(): lax.psum_scatter(down_grad, ('scene', 'seq'), scatter_dimension=0, tiled=...  141 us
    reduce_scatter x1, waiting for transfers between devices, on_device(): lax.psum_scatter(qkv_grad, ('scene', 'seq'), scatter_dimension=0, tiled=T...  125 us
    unnamed x14, waiting for transfers between devices  92.4 us
    all_gather x1, waiting for transfers between devices, on_device(): key_piece = lax.all_gather(key_rows, 'seq', axis=0, tiled=True)  65 us
    all_gather x1, waiting for transfers between devices, on_device(): lax.all_gather(up_part, ('scene', 'seq'), axis=0, tiled=True)  63 us
    all_gather x1, waiting for transfers between devices, on_device(): lax.all_gather(qkv_part, ('scene', 'seq'), axis=0, tiled=True)  63 us
    all_gather x1, waiting for transfers between devices, on_device(): lax.all_gather(down_part, ('scene', 'seq'), axis=0, tiled=True)  59.8 us
  transfers between devices with their start and end apart: 12, of which 12 were waited for; matrix products, arithmetic and copies ran while one was open for 15% of the time, Pallas kernels for 0%

commit v1 on v0

--- a/solution.py
+++ b/solution.py
@@ -6,6 +6,14 @@
 HEADS = 12
 HEAD = 64
 NEG_BIG = -1e30
+
+
+def treat_domain_here(array_here, dim_at):
+    array_here = jnp.moveaxis(array_here, 0, dim_at)
+    view_out = array_here.shape
+    return array_here.reshape(
+        *view_out[:dim_at], view_out[dim_at] * view_out[dim_at + 1], *view_out[dim_at + 2 :]
+    )
 
 
 def norm_rows(values, gain_vector):
@@ -83,7 +91,19 @@
 
     row_max = jnp.full((HEADS, local_rows), NEG_BIG, jnp.float32)
     key_piece = lax.all_gather(key_rows, "seq", axis=0, tiled=True)
-    value_piece = lax.all_gather(value_rows, "seq", axis=0, tiled=True)
+    full_n = lax.axis_size("seq")
+    copies = [(at, (at + 1) % full_n) for at in range(full_n)]
+    rack = [(pp, ii) for ii, pp in copies]
+    lower, f_next = ([], [])
+    for no in tuple(range(full_n - 1)):
+        if no % 2 == 0:
+            lower.append(lax.ppermute(lower[-1] if lower else value_rows, "seq", copies))
+        else:
+            f_next.append(lax.ppermute(f_next[-1] if f_next else value_rows, "seq", rack))
+    e_now = jnp.stack([*lower[::-1], value_rows, *f_next])
+    extra = lax.axis_index("seq") - len(lower)
+    e_now = e_now[(jnp.arange(full_n) - extra) % full_n]
+    value_piece = treat_domain_here(e_now, 0)
     piece_rows = key_piece.shape[0]
     scores = (
         jnp.einsum(

time: 1150 us -> 1160 us (level)
  waiting for transfers between devices: 860 us -> 815 us
  starting transfers between devices: 0.5 us -> 33 us
  local copies, waits for them, and re-layouts: 35 us -> 66.3 us
    ppermute x0 -> x7, waiting for transfers between devices: none -> 75.5 us  [the longest x4 75.5 us: on_device(): lax.ppermute(lower[-1] if lower else value_rows, 'seq', copies)]
    all_gather x1, waiting for transfers between devices: 65 us -> 0.01 us  [on_device(): key_piece = lax.all_gather(key_rows, 'seq', axis=0, tiled=True)]
    ppermute x0 -> x7, starting transfers between devices: none -> 32.3 us  [the longest x3 25.1 us: on_device(): lax.ppermute(f_next[-1] if f_next else value_rows, 'seq', rack)]
    all_gather x1, waiting for transfers between devices: 63 us -> 42.5 us  [on_device(): lax.all_gather(up_part, ('scene', 'seq'), axis=0, tiled=True)]
    all_gather x1, waiting for transfers between devices: 16.4 us -> 0.02 us  [on_device(): lax.all_gather(out_part, ('scene', 'seq'), axis=0, tiled=True)]
    all_gather x1, waiting for transfers between devices: 47.9 us -> 32.9 us  [on_device(): value_piece = lax.all_gather(value_rows, 'seq', axis=0, tiled=True)]
    gather x0 -> x2, local copies, waits for them, and re-layouts: none -> 11.9 us  [on_device(): e_now = e_now[(jnp.arange(full_n) - extra) % full_n]]
    unnamed x58 -> x71, local copies, waits for them, and re-layouts: 20 us -> 30.8 us
  transfers between devices with their start and end apart: 12 -> 19, of which waited for: 12 -> 14; matrix products, arithmetic and copies ran while one was open for 15% -> 21% of each run, Pallas kernels for 0% -> 0%
where the time goes in v1:
time: 1160 us
  waiting for transfers between devices  815 us (70%)
  matrix products  156 us (13%)
  local copies, waits for them, and re-layouts  66.3 us (6%)
  blocking collectives  40.5 us (3%)
  starting transfers between devices  33 us (3%)
  other arithmetic  29.1 us (3%)
  between operations  15.5 us (1%)
    reduce_scatter x1, waiting for transfers between devices, on_device(): lax.psum_scatter(up_grad, ('scene', 'seq'), scatter_dimension=0, tiled=True)  142 us
    reduce_scatter x1, waiting for transfers between devices, on_device(): lax.psum_scatter(down_grad, ('scene', 'seq'), scatter_dimension=0, tiled=...  141 us
    reduce_scatter x1, waiting for transfers between devices, on_device(): lax.psum_scatter(qkv_grad, ('scene', 'seq'), scatter_dimension=0, tiled=T...  125 us
    unnamed x14, waiting for transfers between devices  88.7 us
    ppermute x4, waiting for transfers between devices, on_device(): lax.ppermute(lower[-1] if lower else value_rows, 'seq', copies)  75.5 us
    all_gather x1, waiting for transfers between devices, on_device(): lax.all_gather(qkv_part, ('scene', 'seq'), axis=0, tiled=True)  62.9 us
    all_gather x1, waiting for transfers between devices, on_device(): lax.all_gather(down_part, ('scene', 'seq'), axis=0, tiled=True)  59.8 us
    reduce_scatter x1, waiting for transfers between devices, on_device(): lax.psum_scatter(out_grad, ('scene', 'seq'), scatter_dimension=0, tiled=T...  44.5 us
  transfers between devices with their start and end apart: 19, of which 14 were waited for; matrix products, arithmetic and copies ran while one was open for 21% of the time, Pallas kernels for 0%

profile of v1, /device:TPU:0, one launch (start us, length us, event | category | flops | bytes accessed | tf_op | source)
XLA Modules:
  0.0 1155.7 jit_solution(16727150759837373921)
XLA Ops:
  11.4 62.9 %all-gather.7.cloned.1.call-done = bf16[768,2304]{1,0:T(8,128)(2,1)} async-done(((bf16[24,2304]{1,0:T(8,128)(2,1)}), bf16[768,2304]{1,0:T(8,128)(2,1)}) %all-gather.7.cloned.1.call-update) | async-done | bytes 3538960 | tf_op jit(solution)/shard_map/all_gather | solution.py:72
  82.8 21.0 %collective-permute-done = bf16[320,768]{1,0:T(8,128)(2,1)S(1)} collective-permute-done((bf16[320,768]{1,0:T(8,128)(2,1)S(1)}, bf16[320,768]{1,0:T(8,128)(2,1)S(1)}, u32[]{:S(2)}, u32[]{:S(2)}) %collective-permute-start) | collective-permute-done | bytes 491552 | tf_op jit(solution)/shard_map/ppermute | solution.py:100
  108.5 20.0 %collective-permute-done.1 = bf16[320,768]{1,0:T(8,128)(2,1)S(1)} collective-permute-done((bf16[320,768]{1,0:T(8,128)(2,1)S(1)}, bf16[320,768]{1,0:T(8,128)(2,1)S(1)}, u32[]{:S(2)}, u32[]{:S(2)}) %collective-permute-start.1) | collective-permute-done | bytes 491552 | tf_op jit(solution)/shard_map/ppermute | solution.py:100
  131.5 11.9 %collective-permute-start.5 = (bf16[320,768]{1,0:T(8,128)(2,1)}, bf16[320,768]{1,0:T(8,128)(2,1)}, u32[]{:S(2)}, u32[]{:S(2)}) collective-permute-start(bf16[320,768]{1,0:T(8,128)(2,1)} %collective-permute-done.4), channel_id=1, source_target_pairs={{1,0},{2,1},{3,2},{4,3},{5,4},{6,5},{7,6},{0,7},{9,8},{10,9},{11,1... | collective-permute-start | bytes 1474568 | tf_op jit(solution)/shard_map/ppermute | solution.py:102
  143.5 23.8 %collective-permute-done.2 = bf16[320,768]{1,0:T(8,128)(2,1)} collective-permute-done((bf16[320,768]{1,0:T(8,128)(2,1)S(1)}, bf16[320,768]{1,0:T(8,128)(2,1)}, u32[]{:S(2)}, u32[]{:S(2)}) %collective-permute-start.2) | collective-permute-done | bytes 491552 | tf_op jit(solution)/shard_map/ppermute | solution.py:100
  171.5 8.5 collective-permute-start.6
  180.0 10.7 collective-permute-done.3
  207.2 7.1 copy.31
  214.3 8.0 reshape_reshape.3
  228.6 17.1 %select_reduce_fusion = (f32[12,320]{1,0:T(8,128)S(1)}, f32[12,320,2560]{2,1,0:T(8,128)}) fusion(pred[2560]{0:T(1024)(128)(4,1)S(1)} %fusion.51, bf16[320,12,64]{0,2,1:T(8,128)(2,1)S(1)} %bitcast.70, bf16[2560,12,64]{0,2,1:T(8,128)(2,1)} %bitcast.67), kind=kOutput, calls=%fused_computation.4 | convolution fusion | flops 1287778560 | bytes 43763200 | tf_op jit(solution)/shard_map/qhd,khd->hqk/dot_general | solution.py:109
  245.7 18.1 %fusion = f32[12,320]{1,0:T(8,128)S(1)} fusion(f32[12,320,2560]{2,1,0:T(8,128)} %get-tuple-element.20, f32[12,320]{1,0:T(8,128)S(1)} %broadcast_maximum_fusion, pred[2560]{0:T(1024)(128)(4,1)S(1)} %fusion.51), kind=kLoop, calls=%fused_computation.5 | loop fusion | flops 39317760 | bytes 39354880 | tf_op jit(solution)/shard_map/reduce_sum | solution.py:117
  263.9 15.3 %divide_convert_fusion = bf16[320,12,64]{0,2,1:T(8,128)(2,1)S(1)} fusion(bf16[2560,12,64]{0,2,1:T(8,128)(2,1)S(1)} %copy-done.4, f32[12,320,2560]{2,1,0:T(8,128)} %get-tuple-element.20, f32[12,320]{1,0:T(8,128)S(1)} %broadcast_maximum_fusion, pred[2560]{0:T(1024)(128)(4,1)S(1)} %fusion.51, f32[320,12]{0,1:T(8,128)S(1)} %bitcast.81), kind=kOutput, calls=%fused_computation.36 | convolution fusion | flops 1298104320 | bytes 43778560 | tf_op jit(solution)/shard_map/hqk,khd->hqd/dot_general | solution.py:118
  281.7 42.5 %all-gather.13.cloned.1.call-done = bf16[768,3072]{1,0:T(8,128)(2,1)} async-done(((bf16[24,3072]{1,0:T(8,128)(2,1)}), bf16[768,3072]{1,0:T(8,128)(2,1)}) %all-gather.13.cloned.1.call-update) | async-done | bytes 4718608 | tf_op jit(solution)/shard_map/all_gather | solution.py:74
  330.2 59.8 %all-gather.15.cloned.1.call-done = bf16[3072,768]{1,0:T(8,128)(2,1)} async-done(((bf16[96,768]{1,0:T(8,128)(2,1)}), bf16[3072,768]{1,0:T(8,128)(2,1)}) %all-gather.15.cloned.1.call-update) | async-done | bytes 4718608 | tf_op jit(solution)/shard_map/all_gather | solution.py:75
  390.1 7.9 fusion.18
  403.3 18.3 %fusion.9 = bf16[12,64,2560]{2,1,0:T(8,128)(2,1)} fusion(bf16[320,12,64]{0,2,1:T(8,128)(2,1)} %bitcast.78, f32[12,320,2560]{2,1,0:T(8,128)} %get-tuple-element.20, f32[12,320]{1,0:T(8,128)S(1)} %log_add_fusion, pred[2560]{0:T(1024)(128)(4,1)S(1)} %fusion.51), kind=kOutput, calls=%fused_computation.15 | convolution fusion | flops 1299578880 | bytes 43763200 | tf_op jit(solution)/shard_map/hqk,qhd->khd/dot_general | solution.py:182
  421.7 6.4 copy.36
  428.1 32.9 %all-gather.17.cloned.1.call-done = bf16[2560,768]{1,0:T(8,128)(2,1)} async-done(((bf16[320,768]{1,0:T(8,128)(2,1)}), bf16[2560,768]{1,0:T(8,128)(2,1)}) %all-gather.17.cloned.1.call-update) | async-done | bytes 3932176 | tf_op jit(solution)/shard_map/all_gather | solution.py:164
  461.1 6.3 copy.33
  468.8 26.5 %multiply_convert_fusion = bf16[12,320,2560]{2,1,0:T(8,128)(2,1)} fusion(f32[12,320,2560]{2,1,0:T(8,128)} %get-tuple-element.20, bf16[320,12,64]{0,2,1:T(8,128)(2,1)} %bitcast.80, bf16[2560,12,64]{0,2,1:T(8,128)(2,1)} %bitcast.74, f32[12,320]{1,0:T(8,128)S(1)} %bitcast.82, f32[12,320]{1,0:T(8,128)S(1)} %log_add_fusion, pred[2560]{0:T(1024)(128)(4,1)S(1)} %fusion.51), kind=kOutput, calls=%fused_computation.1 | convolution fusion | flops 1317273600 | bytes 63439360 | tf_op jit(solution)/shard_map/qhd,khd->hqk/dot_general | solution.py:45
  495.3 12.6 %multiply_convert_fusion.1 = bf16[12,64,2560]{2,1,0:T(8,128)(2,1)} fusion(bf16[320,12,64]{0,2,1:T(8,128)(2,1)S(1)} %bitcast.71, bf16[12,320,2560]{2,1,0:T(8,128)(2,1)} %multiply_convert_fusion), kind=kOutput, calls=%fused_computation.12 | convolution fusion | flops 1262223360 | bytes 24084480 | tf_op jit(solution)/shard_map/hqk,qhd->khd/dot_general | solution.py:180
  517.6 6.8 fusion.66
  525.4 8.7 fusion.45
  534.3 10.8 fusion.23
  549.6 86.1 %reduce-scatter.19.cloned.1.call-done = bf16[320,768]{1,0:T(8,128)(2,1)} async-done(((bf16[2560,768]{1,0:T(8,128)(2,1)}), bf16[320,768]{1,0:T(8,128)(2,1)}) %reduce-scatter.19.cloned.1.call-update) | async-done | bytes 491536
  637.8 6.4 fusion.38
  644.2 6.9 fusion.22
  653.0 40.5 %all-reduce.2 = (f32[768]{0:T(1024)S(1)}, f32[768]{0:T(1024)S(1)}) all-reduce(f32[768]{0:T(1024)S(1)} %get-tuple-element.10, f32[768]{0:T(1024)S(1)} %copy-done.26), channel_id=8, replica_groups=mesh['scene'=4,'seq'=8] {'scene','seq'}, use_global_device_ids=true, to_apply=%region_18.19.clone | all-reduce | flops 1536 | bytes 12288
  696.0 44.5 %reduce-scatter.13.cloned.1.call-done = f32[24,768]{1,0:T(8,128)} async-done(((f32[768,768]{1,0:T(8,128)}), f32[24,768]{1,0:T(8,128)}) %reduce-scatter.13.cloned.1.call-update) | async-done | bytes 73744 | tf_op jit(solution)/shard_map/reduce_scatter | solution.py:213
  740.5 141.9 %reduce-scatter.15.cloned.1.call-done = f32[24,3072]{1,0:T(8,128)} async-done(((f32[768,3072]{1,0:T(8,128)}), f32[24,3072]{1,0:T(8,128)}) %reduce-scatter.15.cloned.1.call-update) | async-done | bytes 294928 | tf_op jit(solution)/shard_map/reduce_scatter | solution.py:214
  882.4 141.1 %reduce-scatter.17.cloned.1.call-done = f32[96,768]{1,0:T(8,128)} async-done(((f32[3072,768]{1,0:T(8,128)}), f32[96,768]{1,0:T(8,128)}) %reduce-scatter.17.cloned.1.call-update) | async-done | bytes 294928 | tf_op jit(solution)/shard_map/reduce_scatter | solution.py:215
  1023.5 125.1 %reduce-scatter.11.cloned.1.call-done = f32[24,2304]{1,0:T(8,128)} async-done(((f32[768,2304]{1,0:T(8,128)}), f32[24,2304]{1,0:T(8,128)}) %reduce-scatter.11.cloned.1.call-update) | async-done | bytes 221200 | tf_op jit(solution)/shard_map/reduce_scatter | solution.py:212
  (141 shorter events, 83.5 us)
Async XLA Ops:
  7.2 67.2 %all-gather.7.cloned.1.call-start = ((), (), s32[]{:S(2)}) async-start(), calls=%async_computation.6 | async-start | bytes 3649536 | tf_op jit(solution)/shard_map/all_gather | solution.py:72
  8.8 213.4 %all-gather.9.cloned.1.call-start = ((), (), s32[]{:S(2)}) async-start(), calls=%async_computation.7 | async-start | bytes 4423680 | tf_op jit(solution)/shard_map/all_gather | solution.py:93
  10.1 64.3 %copy-start.19 = (f32[320]{0:T(512)}, f32[320]{0:T(512)S(1)}, u32[]{:S(2)}) copy-start(f32[320]{0:T(512)S(1)} %broadcast_multiply_fusion.5) | copy-start | bytes 3844
  11.4 63.0 %copy-start.21 = (f32[320]{0:T(512)}, f32[320]{0:T(512)S(1)}, u32[]{:S(2)}) copy-start(f32[320]{0:T(512)S(1)} %add_rsqrt_fusion.1) | copy-start | bytes 3844
  11.4 67.5 %copy-start.18 = (f32[24,768]{1,0:T(8,128)S(1)}, f32[24,768]{1,0:T(8,128)}, u32[]{:S(2)}) copy-start(f32[24,768]{1,0:T(8,128)} %param.13) | copy-start | bytes 221188
  11.4 68.3 %copy-start.12 = (f32[24,3072]{1,0:T(8,128)S(1)}, f32[24,3072]{1,0:T(8,128)}, u32[]{:S(2)}) copy-start(f32[24,3072]{1,0:T(8,128)} %param.14) | copy-start | bytes 884740
  78.9 92.6 %copy-start.8 = (bf16[320,768]{1,0:T(8,128)(2,1)}, bf16[320,768]{1,0:T(8,128)(2,1)S(1)}, u32[]{:S(2)}) copy-start(bf16[320,768]{1,0:T(8,128)(2,1)S(1)} %get-tuple-element.17) | copy-start | bytes 1474564
  78.9 200.4 %all-gather.11.cloned.1.call-start = ((), (), s32[]{:S(2)}) async-start(), calls=%async_computation.8 | async-start | bytes 1216512 | tf_op jit(solution)/shard_map/all_gather | solution.py:73
  79.7 244.6 %all-gather.13.cloned.1.call-start = ((), (), s32[]{:S(2)}) async-start(), calls=%async_computation.9 | async-start | bytes 4866048 | tf_op jit(solution)/shard_map/all_gather | solution.py:74
  80.4 309.7 %all-gather.15.cloned.1.call-start = ((), (), s32[]{:S(2)}) async-start(), calls=%async_computation.10 | async-start | bytes 4866048 | tf_op jit(solution)/shard_map/all_gather | solution.py:75
  81.2 379.9 %all-gather.17.cloned.1.call-start = ((), (), s32[]{:S(2)}) async-start(), calls=%async_computation.11 | async-start | bytes 4423680 | tf_op jit(solution)/shard_map/all_gather | solution.py:164
  81.2 22.6 %collective-permute-start = (bf16[320,768]{1,0:T(8,128)(2,1)S(1)}, bf16[320,768]{1,0:T(8,128)(2,1)S(1)}, u32[]{:S(2)}, u32[]{:S(2)}) collective-permute-start(bf16[320,768]{1,0:T(8,128)(2,1)S(1)} %get-tuple-element.17), channel_id=1, source_target_pairs={{0,1},{1,2},{2,3},{3,4},{4,5},{5,6},{6,7},{7,0},{8,9},{9,10},{10,1... | collective-permute-start | bytes 1474568 | tf_op jit(solution)/shard_map/ppermute | solution.py:100
  103.8 24.7 %collective-permute-start.1 = (bf16[320,768]{1,0:T(8,128)(2,1)S(1)}, bf16[320,768]{1,0:T(8,128)(2,1)S(1)}, u32[]{:S(2)}, u32[]{:S(2)}) collective-permute-start(bf16[320,768]{1,0:T(8,128)(2,1)S(1)} %collective-permute-done), channel_id=1, source_target_pairs={{0,1},{1,2},{2,3},{3,4},{4,5},{5,6},{6,7},{7,0},{8,9},{9,10},{10,1... | collective-permute-start | bytes 1474568 | tf_op jit(solution)/shard_map/ppermute | solution.py:100
  103.8 27.8 %collective-permute-start.4 = (bf16[320,768]{1,0:T(8,128)(2,1)S(1)}, bf16[320,768]{1,0:T(8,128)(2,1)}, u32[]{:S(2)}, u32[]{:S(2)}) collective-permute-start(bf16[320,768]{1,0:T(8,128)(2,1)S(1)} %get-tuple-element.17), channel_id=1, source_target_pairs={{1,0},{2,1},{3,2},{4,3},{5,4},{6,5},{7,6},{0,7},{9,8},{10,9},{11,1... | collective-permute-start | bytes 1474568 | tf_op jit(solution)/shard_map/ppermute | solution.py:102
  128.5 42.6 %copy-start.11 = (bf16[320,768]{1,0:T(8,128)(2,1)}, bf16[320,768]{1,0:T(8,128)(2,1)S(1)}, u32[]{:S(2)}) copy-start(bf16[320,768]{1,0:T(8,128)(2,1)S(1)} %collective-permute-done.1) | copy-start | bytes 1474564
  128.5 38.8 %collective-permute-start.2 = (bf16[320,768]{1,0:T(8,128)(2,1)S(1)}, bf16[320,768]{1,0:T(8,128)(2,1)}, u32[]{:S(2)}, u32[]{:S(2)}) collective-permute-start(bf16[320,768]{1,0:T(8,128)(2,1)S(1)} %collective-permute-done.1), channel_id=1, source_target_pairs={{0,1},{1,2},{2,3},{3,4},{4,5},{5,6},{6,7},{7,0},{8,9},{9,10},{10,1... | collective-permute-start | bytes 1474568 | tf_op jit(solution)/shard_map/ppermute | solution.py:100
  131.5 40.0 %collective-permute-start.5 = (bf16[320,768]{1,0:T(8,128)(2,1)}, bf16[320,768]{1,0:T(8,128)(2,1)}, u32[]{:S(2)}, u32[]{:S(2)}) collective-permute-start(bf16[320,768]{1,0:T(8,128)(2,1)} %collective-permute-done.4), channel_id=1, source_target_pairs={{1,0},{2,1},{3,2},{4,3},{5,4},{6,5},{7,6},{0,7},{9,8},{10,9},{11,1... | collective-permute-start | bytes 1474568 | tf_op jit(solution)/shard_map/ppermute | solution.py:102
  167.2 23.5 %collective-permute-start.3 = (bf16[320,768]{1,0:T(8,128)(2,1)}, bf16[320,768]{1,0:T(8,128)(2,1)}, u32[]{:S(2)}, u32[]{:S(2)}) collective-permute-start(bf16[320,768]{1,0:T(8,128)(2,1)} %collective-permute-done.2), channel_id=1, source_target_pairs={{0,1},{1,2},{2,3},{3,4},{4,5},{5,6},{6,7},{7,0},{8,9},{9,10},{10,1... | collective-permute-start | bytes 1474568 | tf_op jit(solution)/shard_map/ppermute | solution.py:100
  171.5 376.0 %reduce-scatter.21.cloned.1.call-start = ((), (), s32[]{:S(2)}) async-start(), calls=%async_computation.17 | async-start | bytes 4423680
  171.5 30.1 %collective-permute-start.6 = (bf16[320,768]{1,0:T(8,128)(2,1)}, bf16[320,768]{1,0:T(8,128)(2,1)S(1)}, u32[]{:S(2)}, u32[]{:S(2)}) collective-permute-start(bf16[320,768]{1,0:T(8,128)(2,1)} %collective-permute-done.5), channel_id=1, source_target_pairs={{1,0},{2,1},{3,2},{4,3},{5,4},{6,5},{7,6},{0,7},{9,8},{10,9},{11,1... | collective-permute-start | bytes 1474568 | tf_op jit(solution)/shard_map/ppermute | solution.py:102
  279.2 51.0 %copy-start.1 = (bf16[320,12,64]{0,2,1:T(8,128)(2,1)}, bf16[320,12,64]{0,2,1:T(8,128)(2,1)S(1)}, u32[]{:S(2)}) copy-start(bf16[320,12,64]{0,2,1:T(8,128)(2,1)S(1)} %divide_convert_fusion) | copy-start | bytes 1474564
  279.2 45.0 %copy-start.15 = (f32[768]{0:T(1024)S(1)}, f32[768]{0:T(1024)}, u32[]{:S(2)}) copy-start(f32[768]{0:T(1024)} %param.17) | copy-start | bytes 9220
  281.7 108.4 %copy-start.9 = (bf16[320,768]{1,0:T(8,128)(2,1)S(1)}, bf16[320,768]{1,0:T(8,128)(2,1)}, u32[]{:S(2)}) copy-start(bf16[320,768]{1,0:T(8,128)(2,1)} %param.11) | copy-start | bytes 1474564
  281.7 108.4 %copy-start.23 = (f32[320]{0:T(512)S(1)}, f32[320]{0:T(512)}, u32[]{:S(2)}) copy-start(f32[320]{0:T(512)} %fusion.55) | copy-start | bytes 3844
  428.1 207.6 %reduce-scatter.19.cloned.1.call-start = ((), (), s32[]{:S(2)}) async-start(), calls=%async_computation.16 | async-start | bytes 4423680
  514.3 226.2 %reduce-scatter.13.cloned.1.call-start = ((), (), s32[]{:S(2)}) async-start(), calls=%async_computation.13 | async-start | bytes 2433024 | tf_op jit(solution)/shard_map/reduce_scatter | solution.py:213
  517.5 364.9 %reduce-scatter.15.cloned.1.call-start = ((), (), s32[]{:S(2)}) async-start(), calls=%async_computation.14 | async-start | bytes 9732096 | tf_op jit(solution)/shard_map/reduce_scatter | solution.py:214
  524.4 499.1 %reduce-scatter.17.cloned.1.call-start = ((), (), s32[]{:S(2)}) async-start(), calls=%async_computation.15 | async-start | bytes 9732096 | tf_op jit(solution)/shard_map/reduce_scatter | solution.py:215
  534.2 103.6 %copy-start.16 = (f32[768]{0:T(1024)S(1)}, f32[768]{0:T(1024)}, u32[]{:S(2)}) copy-start(f32[768]{0:T(1024)} %param.16) | copy-start | bytes 9220
  534.2 103.6 %copy-start.20 = (f32[320]{0:T(512)S(1)}, f32[320]{0:T(512)}, u32[]{:S(2)}) copy-start(f32[320]{0:T(512)} %copy-done.19) | copy-start | bytes 3844
  534.2 103.6 %copy-start.22 = (f32[320]{0:T(512)S(1)}, f32[320]{0:T(512)}, u32[]{:S(2)}) copy-start(f32[320]{0:T(512)} %copy-done.21) | copy-start | bytes 3844
  534.2 614.4 %reduce-scatter.11.cloned.1.call-start = ((), (), s32[]{:S(2)}) async-start(), calls=%async_computation.12 | async-start | bytes 7299072 | tf_op jit(solution)/shard_map/reduce_scatter | solution.py:212
  (16 other events, 111.2 us)
Sparse Core Ops, SparseCore 0:
  11.5 62.8 all-gather.6
  79.0 121.0 all-gather.8
  203.6 54.6 all-gather.10
  261.7 62.5 all-gather.12
  327.6 62.4 all-gather.14
  392.1 68.8 all-gather.16
  464.7 82.7 reduce-scatter.20
  551.6 83.9 reduce-scatter.18
  641.5 98.9 reduce-scatter.12
  747.8 134.5 reduce-scatter.14
  888.9 134.6 reduce-scatter.16
  1030.6 118.0 reduce-scatter.10
